TPU v7x, 1024 devices: a whole 4x8x16 slice. The times are simulated.
1024 devices in a mesh: dp: 8 (over z_hi, x), blk: 16 (over z_lo, core), resp: 8 (over y).
Axes of the slice: x: 4, y: 8, z: 16 (z_hi: 2, z_lo: 8; z = z_hi * 8 + z_lo), core: 2. Of those that a mesh axis runs over, the one named last changes fastest.
Arguments:
- saved: bfloat16 [8, 2048, 3, 1280], P('dp', 'blk', None, 'resp'), may hold values from -24 to 24
- prefix_cot: bfloat16 [8, 8, 2048, 1280], P('dp', 'resp', 'blk'), may hold values from -24 to 24
- w_out: bfloat16 [1280, 1280], P('resp'), may hold values from -0.15625 to 0.15625
- lengths: int32 [8, 16], P('dp', 'resp'), may hold values from 1 to 512, 4096 in all within a row
- adv_mask: int32 [8, 16, 512], P('dp', 'resp'), may hold values from -3 to 3, as said below
- patch_map: int32 [8, 16, 128], P('dp', 'blk'), may hold values from 0 to 127, each once within a row
Outputs:
- grad_qkv: bfloat16 [8, 2048, 3, 1280], P('dp', 'blk', None, 'resp')
Inputs may be any that keep to these rules, and one draw needn't show every extreme that they name: `adv_mask`: within one response every nonzero entry has the same value. The 16 lengths of one image sum to 4096; the longest is 512. `patch_map`: each row of 128 entries holds every number of 0 to 127 once.
All inputs are finite; a program needn't handle non-finite values. No bound on the sum of `lengths` on one device may be relied on, other than what follows from the above.
Results may differ from a plain program's by a relative error of at most 0.03.
Values may be sent and summed in bfloat16 or wider, within the bound.
No kernel may reach another device: no remote copies, remote signals or barrier semaphores. Data moves between devices by JAX's collectives and lax.ppermute only.
A program may use at most 32 MiB of HBM per device.

v0:
```python
import math

import jax
import jax.numpy as jnp
from jax import lax
from jax.sharding import PartitionSpec as P

HD = 80
MAXLEN = 512


def score_pair(query, grad, log_total, delta, keys, values, scale):
    score = jnp.einsum("qhd,khd->hqk", query, keys, preferred_element_type=jnp.float32) * scale
    prob = jnp.exp(score - log_total[:, :, None])
    dprob = jnp.einsum("qhd,khd->hqk", grad, values, preferred_element_type=jnp.float32)
    dscore = (prob * (dprob - delta[:, :, None])).astype(jnp.bfloat16)
    return (prob.astype(jnp.bfloat16), dscore)


def shards(saved, prefix_cot, w_out, lengths, adv_mask, patch_map):
    rows = saved.shape[1]
    width = saved.shape[3]
    heads_here = width // HD
    scale = 1.0 / math.sqrt(HD)
    live = lax.broadcasted_iota(jnp.int32, adv_mask.shape, 2) < lengths[:, :, None]
    resp_weight = jnp.sum(jnp.where(live, adv_mask, 0).astype(jnp.float32), axis=2) / MAXLEN
    group_weight = jnp.sum(resp_weight)
    weighted = group_weight * prefix_cot[0, 0].astype(jnp.float32)
    total = lax.psum(weighted.astype(jnp.bfloat16), "resp")
    cot_rows = jnp.take(total, patch_map[0, 0], axis=0)
    grad_out = lax.dot_general(
        cot_rows, w_out, (((1,), (1,)), ((), ())), preferred_element_type=jnp.float32
    ).astype(jnp.bfloat16)
    query = saved[0, :, 0, :].reshape(rows, heads_here, HD)
    keys = saved[0, :, 1, :].reshape(rows, heads_here, HD)
    values = saved[0, :, 2, :].reshape(rows, heads_here, HD)
    grad = grad_out.reshape(rows, heads_here, HD)
    key_value = saved[0, :, 1:, :].reshape(rows, 2 * width)
    piece = lax.all_gather(key_value, "blk", axis=0, tiled=True)
    top = jnp.full((heads_here, rows), -1e30, jnp.float32)
    count = piece.shape[0]
    key_part = piece[:, :width].reshape(count, heads_here, HD)
    value_part = piece[:, width:].reshape(count, heads_here, HD)
    score = jnp.einsum("qhd,khd->hqk", query, key_part, preferred_element_type=jnp.float32) * scale
    new_top = jnp.maximum(top, jnp.max(score, axis=2))
    expo = jnp.exp(score - new_top[:, :, None])
    row_total = jnp.sum(expo, axis=2)
    accum = jnp.einsum(
        "hqk,khd->hqd", expo.astype(jnp.bfloat16), value_part, preferred_element_type=jnp.float32
    )
    top, row_total, accum = (new_top, row_total, accum)
    output = (accum / row_total[:, :, None]).astype(jnp.bfloat16)
    log_total = top + jnp.log(row_total)
    delta = jnp.einsum("qhd,hqd->hq", grad, output, preferred_element_type=jnp.float32)
    packed = jnp.concatenate([saved[0], grad_out[:, None, :]], axis=1).reshape(rows, 4 * width)
    stats = jnp.concatenate([log_total, delta], axis=0).T
    block = lax.all_gather(packed.astype(jnp.float32), "blk", axis=0, tiled=True).astype(
        jnp.bfloat16
    )
    stat_block = lax.all_gather(stats, "blk", axis=0, tiled=True)
    count = block.shape[0]
    far_q = block[:, :width].reshape(count, heads_here, HD)
    far_k = block[:, width : 2 * width].reshape(count, heads_here, HD)
    far_v = block[:, 2 * width : 3 * width].reshape(count, heads_here, HD)
    far_g = block[:, 3 * width :].reshape(count, heads_here, HD)
    far_log = stat_block[:, :heads_here].T
    far_delta = stat_block[:, heads_here:].T
    near_prob, near_ds = score_pair(query, grad, log_total, delta, far_k, far_v, scale)
    grad_q = jnp.einsum("hqk,khd->hqd", near_ds, far_k, preferred_element_type=jnp.float32) * scale
    far_prob, far_ds = score_pair(far_q, far_g, far_log, far_delta, keys, values, scale)
    grad_k = jnp.einsum("hqk,qhd->khd", far_ds, far_q, preferred_element_type=jnp.float32) * scale
    grad_v = jnp.einsum("hqk,qhd->khd", far_prob, far_g, preferred_element_type=jnp.float32)
    grad_q, grad_k, grad_v = (grad_q, grad_k, grad_v)
    grad_k = grad_k.reshape(rows, width)
    grad_v = grad_v.reshape(rows, width)
    grad_q = grad_q.transpose(1, 0, 2).reshape(rows, width)
    result = jnp.stack([grad_q, grad_k, grad_v], axis=1).astype(jnp.bfloat16)
    return result[None]


def solution(mesh):
    in_specs = (
        P("dp", "blk", None, "resp"),
        P("dp", "resp", "blk", None),
        P("resp", None),
        P("dp", "resp"),
        P("dp", "resp", None),
        P("dp", "blk", None),
    )
    out_specs = P("dp", "blk", None, "resp")
    return jax.shard_map(shards, mesh=mesh, in_specs=in_specs, out_specs=out_specs, check_vma=False)
```

profile of v0, /device:TPU:1, one launch (start us, length us, event | category | flops | bytes accessed | tf_op | source)
XLA Modules:
  0.0 219.3 jit_solution(6501693780212882604)
XLA Ops:
  7.4 0.9 fusion.31
  8.3 0.6 multiply_reduce_fusion
  8.9 2.4 %fusion.26 = bf16[128,1280]{1,0:T(8,128)(2,1)} fusion(bf16[1,1,128,1280]{3,2,1,0:T(8,128)(2,1)} %param.7, f32[]{:T(128)} %multiply_reduce_fusion), kind=kLoop, calls=%fused_computation.36 | loop fusion | flops 491520 | bytes 655364 | tf_op jit(solution)/shard_map/convert_element_type | solution.py:29
  11.4 1.5 slice.38
  13.0 0.7 fusion.32
  13.7 0.7 compare_and_fusion
  14.3 90.6 %all-reduce.2.cloned.1.call-done = bf16[128,1280]{1,0:T(8,128)(2,1)} async-done(((bf16[128,1280]{1,0:T(8,128)(2,1)}), bf16[128,1280]{1,0:T(8,128)(2,1)}) %all-reduce.2.cloned.1.call-update) | async-done | bytes 327696 | tf_op jit(solution)/shard_map/psum | solution.py:29
  104.9 2.2 gather_fusion
  107.1 0.3 convolution_convert_fusion.1
  107.4 0.7 pad_maximum_fusion
  108.1 0.1 copy.12
  108.3 1.4 fusion.35
  109.7 0.6 fusion.37
  110.3 0.4 fusion.10
  110.7 0.6 fusion.18
  111.3 39.2 %all_gather.11 = f32[2048,4]{0,1:T(4,128)S(1)} all-gather(f32[128,4]{0,1:T(4,128)S(1)} %maximum_bitcast_fusion), channel_id=1, replica_groups=mesh['dp'=8,'blk'=16,'resp'=8] {'blk'}, dimensions={0}, use_global_device_ids=true | all-gather | bytes 34816 | tf_op jit(solution)/shard_map/all_gather | solution.py:60
  150.6 49.5 %all-gather.3.cloned.1.call-done = bf16[2048,640]{0,1:T(8,128)(2,1)} async-done(((bf16[128,640]{0,1:T(8,128)(2,1)}), bf16[2048,640]{0,1:T(8,128)(2,1)}) %all-gather.3.cloned.1.call-update) | async-done | bytes 2621456 | tf_op jit(solution)/shard_map/all_gather | solution.py:57
  200.2 2.7 %fusion.34 = (bf16[2048,160]{0,1:T(8,128)(2,1)}, bf16[2048,160]{0,1:T(8,128)(2,1)S(1)}, bf16[2048,160]{0,1:T(8,128)(2,1)S(1)}, bf16[2048,160]{0,1:T(8,128)(2,1)S(1)}) fusion(bf16[2048,640]{0,1:T(8,128)(2,1)} %all-gather.3.cloned.1.call-done), kind=kLoop, calls=%fused_computation.58 | loop fusion | bytes 5242880 | tf_op jit(solution)/shard_map/slice | solution.py:64
  202.9 1.9 fusion.6
  204.8 1.0 fusion.2
  205.9 0.4 convolution_convert_fusion
  206.2 2.4 %fusion.19 = bf16[2,80,128]{2,1,0:T(8,128)(2,1)S(1)} fusion(bf16[2048,2,80]{0,2,1:T(8,128)(2,1)} %bitcast.63, f32[2,2048,128]{2,1,0:T(8,128)S(1)} %fusion.2, bf16[2048,2,80]{0,2,1:T(8,128)(2,1)} %bitcast.65, bf16[128,2,80]{0,2,1:T(8,128)(2,1)S(1)} %bitcast.77, f32[2,2048]{1,0:T(2,128)S(1)} %get-tuple-element.14), kind=kOutput, calls=%fused_computation.27 | convolution fusion | flops 169385984 | bytes 3506176 | tf_op jit(solution)/shard_map/hqk,qhd->khd/dot_general | solution.py:71
  208.6 2.5 %fusion.20 = bf16[2,128,80]{1,2,0:T(8,128)(2,1)S(1)} fusion(bf16[2048,2,80]{0,2,1:T(8,128)(2,1)S(1)} %bitcast.61, f32[2,128,2048]{1,2,0:T(8,128)} %fusion.6, bf16[128,2,80]{0,2,1:T(8,128)(2,1)S(1)} %bitcast.73, bf16[2048,2,80]{0,2,1:T(8,128)(2,1)} %bitcast.67, f32[2,128]{1,0:T(2,128)S(1)} %fusion.18), kind=kOutput, calls=%fused_computation.28 | convolution fusion | flops 169385984 | bytes 3490816 | tf_op jit(solution)/shard_map/hqk,khd->hqd/dot_general | solution.py:69
  211.2 0.7 pad_maximum_fusion.1
  (21 shorter events, 0.2 us)
Async XLA Ops:
  7.4 99.7 %copy-start = (bf16[160,1280]{1,0:T(8,128)(2,1)S(1)}, bf16[160,1280]{1,0:T(8,128)(2,1)}, u32[]{:S(2)}) copy-start(bf16[160,1280]{1,0:T(8,128)(2,1)} %param.8) | copy-start | bytes 1228804
  7.4 97.5 %all-reduce.2.cloned.1.call-start = ((), (), s32[]{:S(2)}) async-start(), calls=%async_computation | async-start | bytes 655360 | tf_op jit(solution)/shard_map/psum | solution.py:29
  11.3 96.1 %copy-start.3 = (bf16[1,128,3,160]{1,3,2,0:T(8,128)(2,1)S(1)}, bf16[1,128,3,160]{1,3,2,0:T(8,128)(2,1)}, u32[]{:S(2)}) copy-start(bf16[1,128,3,160]{1,3,2,0:T(8,128)(2,1)} %param.6) | copy-start | bytes 368644
  11.3 97.0 %all-gather.5.cloned.1.call-start = ((), (), s32[]{:S(2)}) async-start(), calls=%async_computation.2 | async-start | bytes 1392640 | tf_op jit(solution)/shard_map/all_gather | solution.py:39
  12.9 187.2 %all-gather.3.cloned.1.call-start = ((), (), s32[]{:S(2)}) async-start(), calls=%async_computation.1 | async-start | bytes 2785280 | tf_op jit(solution)/shard_map/all_gather | solution.py:57
  202.9 3.0 %copy-start.1 = (bf16[2048,160]{0,1:T(8,128)(2,1)}, bf16[2048,160]{0,1:T(8,128)(2,1)S(1)}, u32[]{:S(2)}) copy-start(bf16[2048,160]{0,1:T(8,128)(2,1)S(1)} %get-tuple-element.6) | copy-start | bytes 1966084
  202.9 3.0 %copy-start.2 = (bf16[2048,160]{0,1:T(8,128)(2,1)}, bf16[2048,160]{0,1:T(8,128)(2,1)S(1)}, u32[]{:S(2)}) copy-start(bf16[2048,160]{0,1:T(8,128)(2,1)S(1)} %get-tuple-element.8) | copy-start | bytes 1966084
Sparse Core Ops, SparseCore 0:
  11.4 93.4 all-reduce.1
Sparse Core Ops, SparseCore 1:
  14.4 91.6 all-gather.4
  108.5 91.6 all-gather.2
where the time goes:
time: 220 us; the launch traced here: 219 us
  waiting for transfers between devices  140 us (64%)
  blocking collectives  39.2 us (18%)
  between operations  15 us (7%)
  matrix products  9.73 us (4%)
  local copies, waits for them, and re-layouts  8.01 us (4%)
  other arithmetic  7.05 us (3%)
    psum x1, waiting for transfers between devices, shards(): total = lax.psum(weighted.astype(jnp.bfloat16), 'resp')  90.6 us
    all_gather x1, waiting for transfers between devices, shards(): lax.all_gather(packed.astype(jnp.float32), 'blk', axis=0, tiled=True)  49.5 us
    all_gather x1, blocking collectives, shards(): stat_block = lax.all_gather(stats, 'blk', axis=0, tiled=True)  39.2 us
  transfers between devices with their start and end apart: 3, of which 2 were waited for; matrix products, arithmetic and copies ran while one was open for 4% of the time, Pallas kernels for 0%

commit v1 on v0

v1 whole, which is shorter than its diff:
```python
import math

import jax
import jax.numpy as jnp
from jax import lax
from jax.experimental import pallas as pl
from jax.experimental.pallas import tpu as pltpu
from jax.sharding import PartitionSpec as P


HD = 80
MAXLEN = 512
LANES = 128
WIDE = 2 * LANES
SCALE = 1.0 / math.sqrt(HD)
SCALE2 = SCALE * math.log2(math.e)
BF = jnp.bfloat16
F32 = jnp.float32

NN = (((1,), (0,)), ((), ()))
NT = (((1,), (1,)), ((), ()))
TN = (((0,), (0,)), ((), ()))


def dot(a, b, dims):
    return lax.dot_general(a, b, dims, preferred_element_type=F32)


def vmem():
    return pl.BlockSpec(memory_space=pltpu.VMEM)


def smem():
    return pl.BlockSpec(memory_space=pltpu.SMEM)


def cost(flops, size):
    return pl.CostEstimate(flops=flops, bytes_accessed=size, transcendentals=0)


def weigh_kernel(len_ref, mask_ref, map_ref, cot_ref, out_ref):
    col = lax.broadcasted_iota(jnp.int32, (1, MAXLEN), 1)
    weight = jnp.zeros((1, 1), F32)
    for r in range(mask_ref.shape[1]):
        live = col < len_ref[0, r]
        marks = jnp.where(live, mask_ref[0, r : r + 1, :], 0).astype(F32)
        weight = weight + jnp.sum(marks, axis=1, keepdims=True) / MAXLEN
    rows = cot_ref.shape[2]
    pick = (lax.broadcasted_iota(jnp.int32, (rows, rows), 0) == map_ref[0]).astype(F32).astype(BF)
    taken = dot(pick, cot_ref[0, 0], TN)
    out_ref[...] = (taken * weight).astype(BF).reshape(out_ref.shape)


def sum_kernel(in_ref, out_ref):
    total = in_ref[0].astype(F32)
    for g in range(1, in_ref.shape[0]):
        total = total + in_ref[g].astype(F32)
    total = total.astype(BF)
    for g in range(out_ref.shape[0]):
        out_ref[g] = total


def grad_kernel(w_ref, rows_ref, out_ref):
    n = rows_ref.shape[0] * rows_ref.shape[1]
    rows = rows_ref[...].reshape(n, rows_ref.shape[2])
    grad = dot(w_ref[...], rows, NT).astype(BF)
    for j in range(out_ref.shape[0]):
        out_ref[j] = grad[(j & 1) * HD : (j & 1) * HD + HD]


def pair(ref, a, b, lo, hi):
    return jnp.concatenate([ref[a, lo:hi, :], ref[b, lo:hi, :]], axis=1)


def forward_kernel(own_ref, oth_ref, kr_ref, vr_ref, kt_ref, out_ref, lse_ref, vt_ref):
    nz = own_ref.shape[0]
    for side, ref in enumerate((own_ref, oth_ref)):
        for s in range(nz):
            span = slice((side * nz + s) * LANES, (side * nz + s + 1) * LANES)
            kr_ref[span, :] = ref[s, HD : 2 * HD, :].T
            vr_ref[span, :] = ref[s, 2 * HD :, :].T
            kt_ref[:, span] = ref[s, HD : 2 * HD, :]
            vt_ref[:, span] = ref[s, 2 * HD :, :]

    def step(j, carry):
        score = dot(kr_ref[...], pair(own_ref, 2 * j, 2 * j + 1, 0, HD), NN)
        top = jnp.max(score, axis=0, keepdims=True)
        expo = jnp.exp2((score - top) * SCALE2)
        total = jnp.sum(expo, axis=0, keepdims=True)
        out = (dot(vt_ref[...], expo.astype(BF), NN) / total).astype(BF)
        lse = top * SCALE2 + jnp.log2(total)
        for e in range(2):
            out_ref[2 * j + e] = out[:, e * LANES : (e + 1) * LANES]
            lse_ref[2 * j + e] = lse[:, e * LANES : (e + 1) * LANES]
        return carry

    lax.fori_loop(0, nz // 2, step, 0)


def backward_kernel(pos_ref, own_ref, kr_ref, vr_ref, kt_ref, o_ref, lse_ref, g_ref, out_ref):
    nz = own_ref.shape[0]
    half = nz * LANES
    chip = pos_ref[0]
    head = pos_ref[1]
    core = pos_ref[2]

    def probs(keys, vals, j):
        a = 2 * j
        query = pair(own_ref, a, a + 1, 0, HD)
        grad = pair(g_ref, chip ^ a, chip ^ (a + 1), 0, HD)
        lse = pair(lse_ref, a, a + 1, 0, 1)
        fwd = pair(o_ref, a, a + 1, 0, HD)
        delta = jnp.sum(grad.astype(F32) * fwd.astype(F32), axis=0, keepdims=True)
        prob = jnp.exp2(dot(keys, query, NN) * SCALE2 - lse)
        dsc = (prob * (dot(vals, grad, NN) - delta)).astype(BF)
        return query, grad, prob.astype(BF), dsc

    _, _, _, dsc = probs(kr_ref[...], vr_ref[...], 0)
    dq = (dot(kt_ref[...], dsc, NN) * SCALE).astype(BF)
    keys = jnp.concatenate([kr_ref[:WIDE, :], kr_ref[half : half + WIDE, :]], axis=0)
    vals = jnp.concatenate([vr_ref[:WIDE, :], vr_ref[half : half + WIDE, :]], axis=0)

    def step(j, acc):
        query, grad, prob, dsc = probs(keys, vals, j)
        return acc[0] + dot(query, dsc, NT), acc[1] + dot(grad, prob, NT)

    zero = jnp.zeros((HD, 2 * WIDE), F32)
    dk, dv = lax.fori_loop(0, nz // 2, step, (zero, zero))
    dk = (dk * SCALE).astype(BF)
    dv = dv.astype(BF)
    for slot in range(2):
        for side in range(2):
            cols = slice(side * WIDE + slot * LANES, side * WIDE + (slot + 1) * LANES)
            dest = 2 * (head ^ slot) + (core ^ side)
            out_ref[dest, :HD, :] = dq[:, slot * LANES : (slot + 1) * LANES]
            out_ref[dest, HD : 2 * HD, :] = dk[:, cols]
            out_ref[dest, 2 * HD :, :] = dv[:, cols]


def make(mesh, interpret=False):
    nresp = mesh.shape["resp"]
    nblk = mesh.shape["blk"]
    nz = nblk // 2
    by_core = [[2 * z + c for z in range(nz)] for c in range(2)]
    quads = [[4 * q + i for i in range(4)] for q in range(nblk // 4)]

    def call(body, outs, n_in, scalars, flops, size, scratch=()):
        in_specs = [smem() if i in scalars else vmem() for i in range(n_in)]
        return pl.pallas_call(
            body,
            out_shape=outs,
            in_specs=in_specs,
            out_specs=jax.tree.map(lambda _: vmem(), outs),
            scratch_shapes=list(scratch),
            cost_estimate=cost(flops, size),
            compiler_params=pltpu.CompilerParams(vmem_limit_bytes=40 * 2**20),
            interpret=interpret,
        )

    def inner(saved, prefix_cot, w_out, lengths, adv_mask, patch_map):
        rows = saved.shape[1]
        model = prefix_cot.shape[3]
        piece = rows // nresp
        sds = jax.ShapeDtypeStruct
        me = lax.axis_index("blk")
        chip, head, core = me >> 1, (me >> 1) & 1, me & 1
        pos = jnp.stack([chip, head, core])

        def hop(x, d):
            return lax.ppermute(x, "blk", [(i, i ^ d) for i in range(nblk)])

        both = saved[0].reshape(rows, 3, 2, HD).transpose(2, 1, 3, 0).reshape(2, 3 * HD, rows)
        mate = hop(lax.dynamic_index_in_dim(both, 1 - head, 0, keepdims=False), 2)

        cot = call(weigh_kernel, sds((nresp, piece, model), BF), 4, (0,), 2 * rows * rows * model, 10**6)(
            lengths, adv_mask, patch_map, prefix_cot
        )
        cot = lax.all_to_all(cot, "resp", 0, 0)
        duo = jnp.stack([lax.dynamic_index_in_dim(both, head, 0, keepdims=False), mate])
        far = [hop(duo, 4 * d) for d in range(1, nz // 2)]
        tot = call(sum_kernel, sds((nresp, piece, model), BF), 1, (), 10**6, 10**6)(cot)
        tot = lax.all_to_all(tot, "resp", 0, 0)
        grad = call(grad_kernel, sds((nz, HD, rows), BF), 2, (), 2 * rows * model * 160, 10**6)(w_out, tot)
        grad = lax.all_to_all(grad, "blk", 0, 0, axis_index_groups=by_core)
        own = jnp.concatenate([duo, *far], axis=0)
        other = hop(own, 1)
        n = nblk * rows
        krows, vrows, kt, fwd, lse = call(
            forward_kernel,
            (
                sds((n, HD), BF),
                sds((n, HD), BF),
                sds((HD, n), BF),
                sds((nz, HD, rows), BF),
                sds((nz, 1, rows), F32),
            ),
            2,
            (),
            4 * n * n * HD,
            4 * 10**6,
            [pltpu.VMEM((HD, n), BF)],
        )(own, other)
        parts = call(backward_kernel, sds((4, 3 * HD, rows), BF), 8, (0,), 5 * n * n * HD, 4 * 10**6)(
            pos, own, krows, vrows, kt, fwd, lse, grad
        )
        parts = lax.all_to_all(parts, "blk", 0, 0, axis_index_groups=quads)

        parts = parts.reshape(2, 2, 3, HD, rows)
        mine = lax.dynamic_index_in_dim(parts[:, :, 0], core, axis=1, keepdims=False)
        sums = (parts[:, 0, 1:].astype(F32) + parts[:, 1, 1:].astype(F32)).astype(BF)
        full = jnp.concatenate([mine[:, None], sums], axis=1)
        return full.transpose(3, 1, 0, 2).reshape(1, rows, 3, 2 * HD)

    in_specs = (
        P("dp", "blk", None, "resp"),
        P("dp", "resp", "blk", None),
        P("resp", None),
        P("dp", "resp"),
        P("dp", "resp", None),
        P("dp", "blk", None),
    )
    out_specs = P("dp", "blk", None, "resp")
    return jax.shard_map(inner, mesh=mesh, in_specs=in_specs, out_specs=out_specs, check_vma=False)


def solution(mesh):
    return make(mesh)
```

time: 220 us -> 95.1 us (0.43)
  waiting for transfers between devices: 140 us -> 18.7 us
  starting transfers between devices: 0.09 us -> 58.8 us
  blocking collectives: 39.2 us -> 0 us
  between operations: 15 us -> 0.14 us
  Pallas kernels: 0 us -> 12.9 us
  matrix products: 9.73 us -> 0 us
  other arithmetic: 7.05 us -> 0.13 us
  local copies, waits for them, and re-layouts: 8.01 us -> 3.77 us
    psum x1 -> x0, waiting for transfers between devices: 90.6 us -> none  [shards(): total = lax.psum(weighted.astype(jnp.bfloat16), 'resp')]
    all_gather x2 -> x0, waiting for transfers between devices: 49.6 us -> none  [the longest x1 49.5 us: shards(): lax.all_gather(packed.astype(jnp.float32), 'blk', axis=0, tiled=True)]
    all_gather x1 -> x0, blocking collectives: 39.2 us -> none  [shards(): stat_block = lax.all_gather(stats, 'blk', axis=0, tiled=True)]
    all_to_all x0 -> x4, starting transfers between devices: none -> 33.2 us  [the longest x1 9.69 us: inner(): grad = lax.all_to_all(grad, 'blk', 0, 0, axis_index_groups=by_core)]
    ppermute x0 -> x5, starting transfers between devices: none -> 25.6 us  [hop(): return lax.ppermute(x, 'blk', [(i, i ^ d) for i in range(nblk)])]
    pallas_call x0 -> x5, Pallas kernels: none -> 12.9 us  [the longest x1 5.29 us: inner(): call(forward_kernel, (sds((n, HD), BF), sds((n, HD), BF), sds((HD, n), BF...]
    all_to_all x0 -> x4, waiting for transfers between devices: none -> 10.5 us  [the longest x1 5.26 us: inner(): grad = lax.all_to_all(grad, 'blk', 0, 0, axis_index_groups=by_core)]
    dot_general x8 -> x0, matrix products: 9.73 us -> none  [the longest x2 2.95 us: score_pair(): jnp.einsum('qhd,khd->hqk', query, keys, preferred_element_type=jnp.float32)]
  transfers between devices with their start and end apart: 3 -> 9, of which waited for: 2 -> 6; matrix products, arithmetic and copies ran while one was open for 4% -> 0% of each run, Pallas kernels for 0% -> 7%
where the time goes in v1:
time: 95.1 us; the launch traced here: 94.4 us
  starting transfers between devices  58.8 us (62%)
  waiting for transfers between devices  18.7 us (20%)
  Pallas kernels  12.9 us (14%)
  local copies, waits for them, and re-layouts  3.77 us (4%)
    ppermute x5, starting transfers between devices, hop(): return lax.ppermute(x, 'blk', [(i, i ^ d) for i in range(nblk)])  25.6 us
    all_to_all x1, starting transfers between devices, inner(): grad = lax.all_to_all(grad, 'blk', 0, 0, axis_index_groups=by_core)  9.69 us
    all_to_all x1, starting transfers between devices, inner(): parts = lax.all_to_all(parts, 'blk', 0, 0, axis_index_groups=quads)  9.07 us
    ppermute x5, waiting for transfers between devices, hop(): return lax.ppermute(x, 'blk', [(i, i ^ d) for i in range(nblk)])  8.14 us
    all_to_all x1, starting transfers between devices, inner(): cot = lax.all_to_all(cot, 'resp', 0, 0)  7.77 us
    all_to_all x1, starting transfers between devices, inner(): tot = lax.all_to_all(tot, 'resp', 0, 0)  6.64 us
    pallas_call x1, Pallas kernels, inner(): call(forward_kernel, (sds((n, HD), BF), sds((n, HD), BF), sds((HD, n), BF...  5.29 us
    all_to_all x1, waiting for transfers between devices, inner(): grad = lax.all_to_all(grad, 'blk', 0, 0, axis_index_groups=by_core)  5.26 us
  transfers between devices with their start and end apart: 9, of which 6 were waited for; matrix products, arithmetic and copies ran while one was open for 0% of the time, Pallas kernels for 7%

profile of v1, /device:TPU:1, one launch (start us, length us, event | category | flops | bytes accessed | tf_op | source)
XLA Modules:
  0.0 94.4 jit_solution(6169147555033436892)
XLA Ops:
  0.0 1.0 %copy-done.1 = bf16[1,1,128,1280]{3,2,1,0:T(8,128)(2,1)S(1)} copy-done((bf16[1,1,128,1280]{3,2,1,0:T(8,128)(2,1)S(1)}, bf16[1,1,128,1280]{3,2,1,0:T(8,128)(2,1)}, u32[]{:S(2)}) %copy-start.1) | copy-done | bytes 327704
  1.0 0.7 copy-done.2
  1.7 0.7 copy-done.3
  2.3 0.7 copy-done.4
  3.0 1.6 %shard_map.65 = bf16[8,16,1280]{2,1,0:T(8,128)(2,1)} custom-call(s32[1,2]{1,0:T(1,128)S(1)} %copy-done.3, s32[1,2,512]{2,1,0:T(2,128)S(1)} %copy-done.2, s32[1,1,128]{2,1,0:T(1,128)S(1)} %copy-done.4, bf16[1,1,128,1280]{3,2,1,0:T(8,128)(2,1)S(1)} %copy-done.1), custom_call_target="tpu_custom_call" | custom-call | flops 41943040 | bytes 1000000 | tf_op jit(solution)/shard_map/pallas_call | solution.py:175
  4.5 7.8 %all-to-all-start = ((bf16[8,16,1280]{2,1,0:T(8,128)(2,1)}), bf16[8,16,1280]{2,1,0:T(8,128)(2,1)S(1)}, u32[]{:S(2)}, u32[]{:S(2)}) async-start(bf16[8,16,1280]{2,1,0:T(8,128)(2,1)} %shard_map.65), calls=%async_computation | async-start | bytes 655360 | tf_op jit(solution)/shard_map/all_to_all | solution.py:178
  12.4 4.0 %collective-permute-start = (bf16[240,128]{1,0:T(8,128)(2,1)S(1)}, bf16[240,128]{1,0:T(8,128)(2,1)S(1)}, u32[]{:S(2)}, u32[]{:S(2)}) collective-permute-start(bf16[240,128]{1,0:T(8,128)(2,1)S(1)} %get-tuple-element.17), channel_id=1, source_target_pairs={{0,16},{8,24},{16,0},{24,8},{32,48},{40,56},{48,32},{56,40},{64,80... | collective-permute-start | bytes 184328 | tf_op jit(solution)/shard_map/ppermute | solution.py:170
  16.4 1.6 %collective-permute-done = bf16[240,128]{1,0:T(8,128)(2,1)S(1)} collective-permute-done((bf16[240,128]{1,0:T(8,128)(2,1)S(1)}, bf16[240,128]{1,0:T(8,128)(2,1)S(1)}, u32[]{:S(2)}, u32[]{:S(2)}) %collective-permute-start) | collective-permute-done | bytes 61472 | tf_op jit(solution)/shard_map/ppermute | solution.py:170
  18.0 14.5 %collective-permute-start.3 = (bf16[2,240,128]{2,1,0:T(8,128)(2,1)S(1)}, bf16[2,240,128]{2,1,0:T(8,128)(2,1)S(1)}, u32[]{:S(2)}, u32[]{:S(2)}) collective-permute-start(bf16[2,240,128]{2,1,0:T(8,128)(2,1)S(1)} %pad_maximum_fusion), channel_id=1, source_target_pairs={{0,96},{8,104},{16,112},{24,120},{32,64},{40,72},{48,80},{56,88},{... | collective-permute-start | bytes 368648 | tf_op jit(solution)/shard_map/ppermute | solution.py:170
  32.5 1.9 %collective-permute-start.2 = (bf16[2,240,128]{2,1,0:T(8,128)(2,1)S(1)}, bf16[2,240,128]{2,1,0:T(8,128)(2,1)S(1)}, u32[]{:S(2)}, u32[]{:S(2)}) collective-permute-start(bf16[2,240,128]{2,1,0:T(8,128)(2,1)S(1)} %pad_maximum_fusion), channel_id=1, source_target_pairs={{0,64},{8,72},{16,80},{24,88},{32,96},{40,104},{48,112},{56,120},{... | collective-permute-start | bytes 368648 | tf_op jit(solution)/shard_map/ppermute | solution.py:170
  34.5 2.2 %collective-permute-start.1 = (bf16[2,240,128]{2,1,0:T(8,128)(2,1)S(1)}, bf16[2,240,128]{2,1,0:T(8,128)(2,1)S(1)}, u32[]{:S(2)}, u32[]{:S(2)}) collective-permute-start(bf16[2,240,128]{2,1,0:T(8,128)(2,1)S(1)} %pad_maximum_fusion), channel_id=1, source_target_pairs={{0,32},{8,40},{16,48},{24,56},{32,0},{40,8},{48,16},{56,24},{64,96... | collective-permute-start | bytes 368648 | tf_op jit(solution)/shard_map/ppermute | solution.py:170
  36.7 0.8 shard_map.66
  37.5 6.6 %all-to-all-start.1 = ((bf16[8,16,1280]{2,1,0:T(8,128)(2,1)}), bf16[8,16,1280]{2,1,0:T(8,128)(2,1)S(1)}, u32[]{:S(2)}, u32[]{:S(2)}) async-start(bf16[8,16,1280]{2,1,0:T(8,128)(2,1)} %shard_map.66), calls=%async_computation.1 | async-start | bytes 655360 | tf_op jit(solution)/shard_map/all_to_all | solution.py:182
  44.1 1.4 %collective-permute-done.1 = bf16[2,240,128]{2,1,0:T(8,128)(2,1)S(1)} collective-permute-done((bf16[2,240,128]{2,1,0:T(8,128)(2,1)S(1)}, bf16[2,240,128]{2,1,0:T(8,128)(2,1)S(1)}, u32[]{:S(2)}, u32[]{:S(2)}) %collective-permute-start.1) | collective-permute-done | bytes 122912 | tf_op jit(solution)/shard_map/ppermute | solution.py:170
  45.5 5.2 %collective-permute-done.2 = bf16[2,240,128]{2,1,0:T(8,128)(2,1)S(1)} collective-permute-done((bf16[2,240,128]{2,1,0:T(8,128)(2,1)S(1)}, bf16[2,240,128]{2,1,0:T(8,128)(2,1)S(1)}, u32[]{:S(2)}, u32[]{:S(2)}) %collective-permute-start.2) | collective-permute-done | bytes 122912 | tf_op jit(solution)/shard_map/ppermute | solution.py:170
  50.7 3.0 %collective-permute-start.4 = (bf16[8,240,128]{2,1,0:T(8,128)(2,1)S(1)}, bf16[8,240,128]{2,1,0:T(8,128)(2,1)S(1)}, u32[]{:S(2)}, u32[]{:S(2)}) collective-permute-start(bf16[8,240,128]{2,1,0:T(8,128)(2,1)S(1)} %constant_dynamic-update-slice_fusion.own_ref), channel_id=1, source_target_pairs={{0,8},{8,0},{16,24},{24,16},{32,40},{40,32},{48,56},{56,48},{64,72... | collective-permute-start | bytes 1474568 | tf_op jit(solution)/shard_map/ppermute | solution.py:170
  54.1 0.9 shard_map.67
  55.1 9.7 %all-to-all-start.2 = ((bf16[8,80,128]{2,1,0:T(8,128)(2,1)}), bf16[8,80,128]{2,1,0:T(8,128)(2,1)S(1)}, u32[]{:S(2)}, u32[]{:S(2)}) async-start(bf16[8,80,128]{2,1,0:T(8,128)(2,1)} %shard_map.67), calls=%async_computation.2 | async-start | bytes 327680 | tf_op jit(solution)/shard_map/all_to_all | solution.py:184
  64.8 5.3 %shard_map.64 = (bf16[2048,80]{1,0:T(8,128)(2,1)S(1)}, bf16[2048,80]{1,0:T(8,128)(2,1)S(1)}, bf16[80,2048]{1,0:T(8,128)(2,1)S(1)}, bf16[8,80,128]{2,1,0:T(8,128)(2,1)S(1)}, f32[8,1,128]{2,1,0:T(1,128)S(1)}) custom-call(bf16[8,240,128]{2,1,0:T(8,128)(2,1)S(1)} %constant_dynamic-update-slice_fusion.own_ref, bf16[8,240,128]{2,1,0:T(8,128)(2,1)S(1)} %collective-permute-done.4.oth_ref), custom_call_target="tpu_custom_call" | custom-call | flops 1342177280 | bytes 4000000 | tf_op jit(solution)/shard_map/pallas_call | solution.py:188
  70.1 5.3 %all-to-all-done.2.g_ref = bf16[8,80,128]{2,1,0:T(8,128)(2,1)S(1)} async-done(((bf16[8,80,128]{2,1,0:T(8,128)(2,1)}), bf16[8,80,128]{2,1,0:T(8,128)(2,1)S(1)}, u32[]{:S(2)}, u32[]{:S(2)}) %all-to-all-start.2) | async-done | bytes 163872 | tf_op jit(solution)/shard_map/all_to_all | solution.py:184
  75.4 4.3 %shard_map.68 = bf16[4,240,128]{2,1,0:T(8,128)(2,1)} custom-call(s32[3]{0:T(128)S(1)} %pad_add_fusion.pos_ref, bf16[8,240,128]{2,1,0:T(8,128)(2,1)S(1)} %constant_dynamic-update-slice_fusion.own_ref, bf16[2048,80]{1,0:T(8,128)(2,1)S(1)} %get-tuple-element.10.kr_ref, bf16[2048,80]{1,0:T(8,128)(2,1)S(1)} %get-tuple-element.11.vr_ref, ...), custom_call_target="tpu_custom_call" | custom-call | flops 1677721600 | bytes 4000000 | tf_op jit(solution)/shard_map/pallas_call | solution.py:203
  79.7 9.1 %all-to-all-start.3 = ((bf16[4,240,128]{2,1,0:T(8,128)(2,1)}), bf16[4,240,128]{2,1,0:T(8,128)(2,1)S(1)}, u32[]{:S(2)}, u32[]{:S(2)}) async-start(bf16[4,240,128]{2,1,0:T(8,128)(2,1)} %shard_map.68), calls=%async_computation.3 | async-start | bytes 491520 | tf_op jit(solution)/shard_map/all_to_all | solution.py:206
  88.8 4.9 %all-to-all-done.3 = bf16[4,240,128]{2,1,0:T(8,128)(2,1)S(1)} async-done(((bf16[4,240,128]{2,1,0:T(8,128)(2,1)}), bf16[4,240,128]{2,1,0:T(8,128)(2,1)S(1)}, u32[]{:S(2)}, u32[]{:S(2)}) %all-to-all-start.3) | async-done | bytes 245792 | tf_op jit(solution)/shard_map/all_to_all | solution.py:206
  93.7 0.7 copy.8
  (24 shorter events, 0.7 us)
Async XLA Ops:
  0.0 1.0 %copy-start.1 = (bf16[1,1,128,1280]{3,2,1,0:T(8,128)(2,1)S(1)}, bf16[1,1,128,1280]{3,2,1,0:T(8,128)(2,1)}, u32[]{:S(2)}) copy-start(bf16[1,1,128,1280]{3,2,1,0:T(8,128)(2,1)} %cot_ref.1) | copy-start | bytes 983044
  1.0 0.7 copy-start.2
  1.7 0.7 copy-start.3
  2.3 0.7 copy-start.4
  4.5 7.8 %copy-start.5 = (bf16[1,128,3,160]{1,3,2,0:T(8,128)(2,1)S(1)}, bf16[1,128,3,160]{1,3,2,0:T(8,128)(2,1)}, u32[]{:S(2)}) copy-start(bf16[1,128,3,160]{1,3,2,0:T(8,128)(2,1)} %param.6) | copy-start | bytes 368644
  4.5 32.1 %all-to-all-start = ((bf16[8,16,1280]{2,1,0:T(8,128)(2,1)}), bf16[8,16,1280]{2,1,0:T(8,128)(2,1)S(1)}, u32[]{:S(2)}, u32[]{:S(2)}) async-start(bf16[8,16,1280]{2,1,0:T(8,128)(2,1)} %shard_map.65), calls=%async_computation | async-start | bytes 655360 | tf_op jit(solution)/shard_map/all_to_all | solution.py:178
  12.4 5.6 %collective-permute-start = (bf16[240,128]{1,0:T(8,128)(2,1)S(1)}, bf16[240,128]{1,0:T(8,128)(2,1)S(1)}, u32[]{:S(2)}, u32[]{:S(2)}) collective-permute-start(bf16[240,128]{1,0:T(8,128)(2,1)S(1)} %get-tuple-element.17), channel_id=1, source_target_pairs={{0,16},{8,24},{16,0},{24,8},{32,48},{40,56},{48,32},{56,40},{64,80... | collective-permute-start | bytes 184328 | tf_op jit(solution)/shard_map/ppermute | solution.py:170
  18.0 32.7 %collective-permute-start.3 = (bf16[2,240,128]{2,1,0:T(8,128)(2,1)S(1)}, bf16[2,240,128]{2,1,0:T(8,128)(2,1)S(1)}, u32[]{:S(2)}, u32[]{:S(2)}) collective-permute-start(bf16[2,240,128]{2,1,0:T(8,128)(2,1)S(1)} %pad_maximum_fusion), channel_id=1, source_target_pairs={{0,96},{8,104},{16,112},{24,120},{32,64},{40,72},{48,80},{56,88},{... | collective-permute-start | bytes 368648 | tf_op jit(solution)/shard_map/ppermute | solution.py:170
  32.5 18.1 %collective-permute-start.2 = (bf16[2,240,128]{2,1,0:T(8,128)(2,1)S(1)}, bf16[2,240,128]{2,1,0:T(8,128)(2,1)S(1)}, u32[]{:S(2)}, u32[]{:S(2)}) collective-permute-start(bf16[2,240,128]{2,1,0:T(8,128)(2,1)S(1)} %pad_maximum_fusion), channel_id=1, source_target_pairs={{0,64},{8,72},{16,80},{24,88},{32,96},{40,104},{48,112},{56,120},{... | collective-permute-start | bytes 368648 | tf_op jit(solution)/shard_map/ppermute | solution.py:170
  34.5 11.0 %collective-permute-start.1 = (bf16[2,240,128]{2,1,0:T(8,128)(2,1)S(1)}, bf16[2,240,128]{2,1,0:T(8,128)(2,1)S(1)}, u32[]{:S(2)}, u32[]{:S(2)}) collective-permute-start(bf16[2,240,128]{2,1,0:T(8,128)(2,1)S(1)} %pad_maximum_fusion), channel_id=1, source_target_pairs={{0,32},{8,40},{16,48},{24,56},{32,0},{40,8},{48,16},{56,24},{64,96... | collective-permute-start | bytes 368648 | tf_op jit(solution)/shard_map/ppermute | solution.py:170
  37.5 16.7 %all-to-all-start.1 = ((bf16[8,16,1280]{2,1,0:T(8,128)(2,1)}), bf16[8,16,1280]{2,1,0:T(8,128)(2,1)S(1)}, u32[]{:S(2)}, u32[]{:S(2)}) async-start(bf16[8,16,1280]{2,1,0:T(8,128)(2,1)} %shard_map.66), calls=%async_computation.1 | async-start | bytes 655360 | tf_op jit(solution)/shard_map/all_to_all | solution.py:182
  44.1 10.0 %copy-start = (bf16[160,1280]{1,0:T(8,128)(2,1)S(1)}, bf16[160,1280]{1,0:T(8,128)(2,1)}, u32[]{:S(2)}) copy-start(bf16[160,1280]{1,0:T(8,128)(2,1)} %w_ref.1) | copy-start | bytes 1228804
  50.7 14.1 %collective-permute-start.4 = (bf16[8,240,128]{2,1,0:T(8,128)(2,1)S(1)}, bf16[8,240,128]{2,1,0:T(8,128)(2,1)S(1)}, u32[]{:S(2)}, u32[]{:S(2)}) collective-permute-start(bf16[8,240,128]{2,1,0:T(8,128)(2,1)S(1)} %constant_dynamic-update-slice_fusion.own_ref), channel_id=1, source_target_pairs={{0,8},{8,0},{16,24},{24,16},{32,40},{40,32},{48,56},{56,48},{64,72... | collective-permute-start | bytes 1474568 | tf_op jit(solution)/shard_map/ppermute | solution.py:170
  55.1 20.3 %all-to-all-start.2 = ((bf16[8,80,128]{2,1,0:T(8,128)(2,1)}), bf16[8,80,128]{2,1,0:T(8,128)(2,1)S(1)}, u32[]{:S(2)}, u32[]{:S(2)}) async-start(bf16[8,80,128]{2,1,0:T(8,128)(2,1)} %shard_map.67), calls=%async_computation.2 | async-start | bytes 327680 | tf_op jit(solution)/shard_map/all_to_all | solution.py:184
  79.7 13.9 %all-to-all-start.3 = ((bf16[4,240,128]{2,1,0:T(8,128)(2,1)}), bf16[4,240,128]{2,1,0:T(8,128)(2,1)S(1)}, u32[]{:S(2)}, u32[]{:S(2)}) async-start(bf16[4,240,128]{2,1,0:T(8,128)(2,1)} %shard_map.68), calls=%async_computation.3 | async-start | bytes 491520 | tf_op jit(solution)/shard_map/all_to_all | solution.py:206

commit v2 on v1

--- a/solution.py
+++ b/solution.py
@@ -38,15 +38,26 @@
     return pl.CostEstimate(flops=flops, bytes_accessed=size, transcendentals=0)
 
 
-def weigh_kernel(len_ref, mask_ref, map_ref, cot_ref, out_ref):
+def weigh_kernel(len_hbm, mask_hbm, map_hbm, cot_hbm, out_ref, len_ref, mask_ref, map_ref, cot_ref, sems):
+    loads = [
+        pltpu.make_async_copy(src, dst, sems.at[n])
+        for n, (src, dst) in enumerate(
+            ((cot_hbm, cot_ref), (mask_hbm, mask_ref), (map_hbm, map_ref), (len_hbm, len_ref))
+        )
+    ]
+    for load in loads:
+        load.start()
+    for load in loads[1:]:
+        load.wait()
     col = lax.broadcasted_iota(jnp.int32, (1, MAXLEN), 1)
     weight = jnp.zeros((1, 1), F32)
     for r in range(mask_ref.shape[1]):
-        live = col < len_ref[0, r]
+        live = col < len_ref[0:1, r : r + 1]
         marks = jnp.where(live, mask_ref[0, r : r + 1, :], 0).astype(F32)
         weight = weight + jnp.sum(marks, axis=1, keepdims=True) / MAXLEN
     rows = cot_ref.shape[2]
     pick = (lax.broadcasted_iota(jnp.int32, (rows, rows), 0) == map_ref[0]).astype(F32).astype(BF)
+    loads[0].wait()
     taken = dot(pick, cot_ref[0, 0], TN)
     out_ref[...] = (taken * weight).astype(BF).reshape(out_ref.shape)
 
@@ -107,7 +118,8 @@
     def probs(keys, vals, j):
         a = 2 * j
         query = pair(own_ref, a, a + 1, 0, HD)
-        grad = pair(g_ref, chip ^ a, chip ^ (a + 1), 0, HD)
+        src = chip ^ (4 * (j & 1) + 2 * (j >> 1))
+        grad = pair(g_ref, src, src ^ 1, 0, HD)
         lse = pair(lse_ref, a, a + 1, 0, 1)
         fwd = pair(o_ref, a, a + 1, 0, HD)
         delta = jnp.sum(grad.astype(F32) * fwd.astype(F32), axis=0, keepdims=True)
@@ -137,6 +149,17 @@
             out_ref[dest, 2 * HD :, :] = dv[:, cols]
 
 
+def finish_kernel(pos_ref, in_ref, out_ref):
+    core = pos_ref[2]
+    for p in range(2):
+        span = slice(p * HD, (p + 1) * HD)
+        out_ref[0, span, :] = in_ref[2 * p + core, :HD, :]
+        for t in range(1, 3):
+            rows = slice(t * HD, (t + 1) * HD)
+            a, b = in_ref[2 * p, rows, :], in_ref[2 * p + 1, rows, :]
+            out_ref[t, span, :] = (a.astype(F32) + b.astype(F32)).astype(BF)
+
+
 def make(mesh, interpret=False):
     nresp = mesh.shape["resp"]
     nblk = mesh.shape["blk"]
@@ -144,8 +167,10 @@
     by_core = [[2 * z + c for z in range(nz)] for c in range(2)]
     quads = [[4 * q + i for i in range(4)] for q in range(nblk // 4)]
 
-    def call(body, outs, n_in, scalars, flops, size, scratch=()):
+    def call(body, outs, n_in, scalars, flops, size, scratch=(), raw=False):
         in_specs = [smem() if i in scalars else vmem() for i in range(n_in)]
+        if raw:
+            in_specs = [pl.BlockSpec(memory_space=pltpu.HBM)] * n_in
         return pl.pallas_call(
             body,
             out_shape=outs,
@@ -153,7 +178,7 @@
             out_specs=jax.tree.map(lambda _: vmem(), outs),
             scratch_shapes=list(scratch),
             cost_estimate=cost(flops, size),
-            compiler_params=pltpu.CompilerParams(vmem_limit_bytes=40 * 2**20),
+            compiler_params=pltpu.CompilerParams(vmem_limit_bytes=(63 if raw else 40) * 2**20),
             interpret=interpret,
         )
 
@@ -169,20 +194,31 @@
         def hop(x, d):
             return lax.ppermute(x, "blk", [(i, i ^ d) for i in range(nblk)])
 
-        both = saved[0].reshape(rows, 3, 2, HD).transpose(2, 1, 3, 0).reshape(2, 3 * HD, rows)
-        mate = hop(lax.dynamic_index_in_dim(both, 1 - head, 0, keepdims=False), 2)
-
-        cot = call(weigh_kernel, sds((nresp, piece, model), BF), 4, (0,), 2 * rows * rows * model, 10**6)(
-            lengths, adv_mask, patch_map, prefix_cot
-        )
+        stage = [
+            pltpu.VMEM(lengths.shape, jnp.int32),
+            pltpu.VMEM(adv_mask.shape, jnp.int32),
+            pltpu.VMEM(patch_map.shape, jnp.int32),
+            pltpu.VMEM(prefix_cot.shape, BF),
+            pltpu.SemaphoreType.DMA((4,)),
+        ]
+        cot = call(
+            weigh_kernel, sds((nresp, piece, model), BF), 4, (), 2 * rows * rows * model, 10**6, stage, True
+        )(lengths, adv_mask, patch_map, prefix_cot)
         cot = lax.all_to_all(cot, "resp", 0, 0)
-        duo = jnp.stack([lax.dynamic_index_in_dim(both, head, 0, keepdims=False), mate])
-        far = [hop(duo, 4 * d) for d in range(1, nz // 2)]
+        both = saved[0].transpose(1, 2, 0)
+        lo, hi = both[:, :HD], both[:, HD:]
+        kept = jnp.where(head == 0, lo, hi).reshape(3 * HD, rows)
+        sent = jnp.where(head == 0, hi, lo).reshape(3 * HD, rows)
+        mate = hop(sent, 2)
+        duo = jnp.stack([kept, mate])
+        quad = hop(duo, 8)
+        quad = jnp.concatenate([duo, quad])
+        octo = hop(quad, 4)
         tot = call(sum_kernel, sds((nresp, piece, model), BF), 1, (), 10**6, 10**6)(cot)
         tot = lax.all_to_all(tot, "resp", 0, 0)
         grad = call(grad_kernel, sds((nz, HD, rows), BF), 2, (), 2 * rows * model * 160, 10**6)(w_out, tot)
         grad = lax.all_to_all(grad, "blk", 0, 0, axis_index_groups=by_core)
-        own = jnp.concatenate([duo, *far], axis=0)
+        own = jnp.concatenate([quad, octo])
         other = hop(own, 1)
         n = nblk * rows
         krows, vrows, kt, fwd, lse = call(
@@ -205,11 +241,8 @@
         )
         parts = lax.all_to_all(parts, "blk", 0, 0, axis_index_groups=quads)
 
-        parts = parts.reshape(2, 2, 3, HD, rows)
-        mine = lax.dynamic_index_in_dim(parts[:, :, 0], core, axis=1, keepdims=False)
-        sums = (parts[:, 0, 1:].astype(F32) + parts[:, 1, 1:].astype(F32)).astype(BF)
-        full = jnp.concatenate([mine[:, None], sums], axis=1)
-        return full.transpose(3, 1, 0, 2).reshape(1, rows, 3, 2 * HD)
+        out = call(finish_kernel, sds((3, 2 * HD, rows), BF), 2, (0,), 10**5, 10**6)(pos, parts)
+        return out.transpose(2, 0, 1)[None]
 
     in_specs = (
         P("dp", "blk", None, "resp"),

time: 95.1 us -> 90.9 us (0.956)
  blocking collectives: 0 us -> 10.1 us
  waiting for transfers between devices: 18.7 us -> 11.2 us
  starting transfers between devices: 58.8 us -> 54.9 us
  local copies, waits for them, and re-layouts: 3.77 us -> 0.01 us
    all_to_all x0 -> x1, blocking collectives: none -> 10.1 us  [inner(): parts = lax.all_to_all(parts, 'blk', 0, 0, axis_index_groups=quads)]
    all_to_all x1 -> x0, starting transfers between devices: 9.07 us -> none  [inner(): parts = lax.all_to_all(parts, 'blk', 0, 0, axis_index_groups=quads)]
    ppermute x5 -> x4, starting transfers between devices: 25.6 us -> 31.1 us  [hop(): return lax.ppermute(x, 'blk', [(i, i ^ d) for i in range(nblk)])]
    all_to_all x1 -> x0, waiting for transfers between devices: 4.87 us -> none  [inner(): parts = lax.all_to_all(parts, 'blk', 0, 0, axis_index_groups=quads)]
    unnamed x16 -> x4, local copies, waits for them, and re-layouts: 3.06 us -> 0.01 us
    ppermute x5 -> x4, waiting for transfers between devices: 8.14 us -> 5.48 us  [hop(): return lax.ppermute(x, 'blk', [(i, i ^ d) for i in range(nblk)])]
    pallas_call x1 -> x2, Pallas kernels: 1.56 us -> 3.21 us  [the longest x1 2 us: inner(): call(weigh_kernel, sds((nresp, piece, model), BF), 4, (), 2 * rows * rows...]
  transfers between devices with their start and end apart: 9 -> 7, of which waited for: 6 -> 3; matrix products, arithmetic and copies ran while one was open for 0% -> 0% of each run, Pallas kernels for 7% -> 8%
where the time goes in v2:
time: 90.9 us; the launch traced here: 90.3 us
  starting transfers between devices  54.9 us (60%)
  Pallas kernels  13.8 us (15%)
  waiting for transfers between devices  11.2 us (12%)
  blocking collectives  10.1 us (11%)
    ppermute x4, starting transfers between devices, hop(): return lax.ppermute(x, 'blk', [(i, i ^ d) for i in range(nblk)])  31.1 us
    all_to_all x1, blocking collectives, inner(): parts = lax.all_to_all(parts, 'blk', 0, 0, axis_index_groups=quads)  10.1 us
    all_to_all x1, starting transfers between devices, inner(): grad = lax.all_to_all(grad, 'blk', 0, 0, axis_index_groups=by_core)  9.43 us
    all_to_all x1, starting transfers between devices, inner(): cot = lax.all_to_all(cot, 'resp', 0, 0)  7.78 us
    all_to_all x1, starting transfers between devices, inner(): tot = lax.all_to_all(tot, 'resp', 0, 0)  6.64 us
    all_to_all x1, waiting for transfers between devices, inner(): grad = lax.all_to_all(grad, 'blk', 0, 0, axis_index_groups=by_core)  5.73 us
    ppermute x4, waiting for transfers between devices, hop(): return lax.ppermute(x, 'blk', [(i, i ^ d) for i in range(nblk)])  5.48 us
    pallas_call x1, Pallas kernels, inner(): call(forward_kernel, (sds((n, HD), BF), sds((n, HD), BF), sds((HD, n), BF...  5.27 us
  transfers between devices with their start and end apart: 7, of which 3 were waited for; matrix products, arithmetic and copies ran while one was open for 0% of the time, Pallas kernels for 8%

profile of v2, /device:TPU:1, one launch (start us, length us, event | category | flops | bytes accessed | tf_op | source)
XLA Modules:
  0.0 90.3 jit_solution(1805592349272999884)
XLA Ops:
  0.0 2.0 %shard_map.65 = bf16[8,16,1280]{2,1,0:T(8,128)(2,1)} custom-call(s32[1,2]{1,0:T(1,128)} %len_hbm.1, s32[1,2,512]{2,1,0:T(2,128)} %mask_hbm.1, s32[1,1,128]{2,1,0:T(1,128)} %map_hbm.1, bf16[1,1,128,1280]{3,2,1,0:T(8,128)(2,1)} %cot_hbm.1), custom_call_target="tpu_custom_call" | custom-call | flops 41943040 | bytes 1000000 | tf_op jit(solution)/shard_map/pallas_call | solution.py:204
  2.0 0.0 copy-start.1
  2.0 7.8 %all-to-all-start = ((bf16[8,16,1280]{2,1,0:T(8,128)(2,1)}), bf16[8,16,1280]{2,1,0:T(8,128)(2,1)S(1)}, u32[]{:S(2)}, u32[]{:S(2)}) async-start(bf16[8,16,1280]{2,1,0:T(8,128)(2,1)} %shard_map.65), calls=%async_computation | async-start | bytes 655360 | tf_op jit(solution)/shard_map/all_to_all | solution.py:207
  9.8 4.0 %collective-permute-start = (bf16[240,128]{1,0:T(8,128)(2,1)S(1)}, bf16[240,128]{1,0:T(8,128)(2,1)S(1)}, u32[]{:S(2)}, u32[]{:S(2)}) collective-permute-start(bf16[240,128]{1,0:T(8,128)(2,1)S(1)} %bitcast.19), channel_id=1, source_target_pairs={{0,16},{8,24},{16,0},{24,8},{32,48},{40,56},{48,32},{56,40},{64,80... | collective-permute-start | bytes 184328 | tf_op jit(solution)/shard_map/ppermute | solution.py:195
  13.8 1.6 %collective-permute-done = bf16[240,128]{1,0:T(8,128)(2,1)S(1)} collective-permute-done((bf16[240,128]{1,0:T(8,128)(2,1)S(1)}, bf16[240,128]{1,0:T(8,128)(2,1)S(1)}, u32[]{:S(2)}, u32[]{:S(2)}) %collective-permute-start) | collective-permute-done | bytes 61472 | tf_op jit(solution)/shard_map/ppermute | solution.py:195
  15.5 10.9 %collective-permute-start.1 = (bf16[2,240,128]{2,1,0:T(8,128)(2,1)S(1)}, bf16[2,240,128]{2,1,0:T(8,128)(2,1)S(1)}, u32[]{:S(2)}, u32[]{:S(2)}) collective-permute-start(bf16[2,240,128]{2,1,0:T(8,128)(2,1)S(1)} %pad_maximum_fusion.2), channel_id=1, source_target_pairs={{0,64},{8,72},{16,80},{24,88},{32,96},{40,104},{48,112},{56,120},{... | collective-permute-start | bytes 368648 | tf_op jit(solution)/shard_map/ppermute | solution.py:195
  26.4 0.0 all-to-all-done.in_ref
  26.4 0.8 shard_map.66
  27.2 6.6 %all-to-all-start.1 = ((bf16[8,16,1280]{2,1,0:T(8,128)(2,1)}), bf16[8,16,1280]{2,1,0:T(8,128)(2,1)S(1)}, u32[]{:S(2)}, u32[]{:S(2)}) async-start(bf16[8,16,1280]{2,1,0:T(8,128)(2,1)} %shard_map.66), calls=%async_computation.1 | async-start | bytes 655360 | tf_op jit(solution)/shard_map/all_to_all | solution.py:218
  33.8 0.0 collective-permute-done.1
  33.8 0.0 copy-start
  33.9 5.9 %collective-permute-start.2 = (bf16[4,240,128]{2,1,0:T(8,128)(2,1)S(1)}, bf16[4,240,128]{2,1,0:T(8,128)(2,1)S(1)}, u32[]{:S(2)}, u32[]{:S(2)}) collective-permute-start(bf16[4,240,128]{2,1,0:T(8,128)(2,1)S(1)} %pad_maximum_fusion.1), channel_id=1, source_target_pairs={{0,32},{8,40},{16,48},{24,56},{32,0},{40,8},{48,16},{56,24},{64,96... | collective-permute-start | bytes 737288 | tf_op jit(solution)/shard_map/ppermute | solution.py:195
  39.8 3.9 %collective-permute-done.2 = bf16[4,240,128]{2,1,0:T(8,128)(2,1)S(1)} collective-permute-done((bf16[4,240,128]{2,1,0:T(8,128)(2,1)S(1)}, bf16[4,240,128]{2,1,0:T(8,128)(2,1)S(1)}, u32[]{:S(2)}, u32[]{:S(2)}) %collective-permute-start.2) | collective-permute-done | bytes 245792 | tf_op jit(solution)/shard_map/ppermute | solution.py:195
  43.7 0.1 pad_maximum_fusion.own_ref
  43.7 10.2 %collective-permute-start.3 = (bf16[8,240,128]{2,1,0:T(8,128)(2,1)S(1)}, bf16[8,240,128]{2,1,0:T(8,128)(2,1)S(1)}, u32[]{:S(2)}, u32[]{:S(2)}) collective-permute-start(bf16[8,240,128]{2,1,0:T(8,128)(2,1)S(1)} %pad_maximum_fusion.own_ref), channel_id=1, source_target_pairs={{0,8},{8,0},{16,24},{24,16},{32,40},{40,32},{48,56},{56,48},{64,72... | collective-permute-start | bytes 1474568 | tf_op jit(solution)/shard_map/ppermute | solution.py:195
  53.9 0.0 all-to-all-done.1.rows_ref
  54.0 0.9 %shard_map.67 = bf16[8,80,128]{2,1,0:T(8,128)(2,1)} custom-call(bf16[160,1280]{1,0:T(8,128)(2,1)S(1)} %copy-done, bf16[8,16,1280]{2,1,0:T(8,128)(2,1)S(1)} %all-to-all-done.1.rows_ref), custom_call_target="tpu_custom_call" | custom-call | flops 52428800 | bytes 1000000 | tf_op jit(solution)/shard_map/pallas_call | solution.py:219
  54.9 9.4 %all-to-all-start.2 = ((bf16[8,80,128]{2,1,0:T(8,128)(2,1)}), bf16[8,80,128]{2,1,0:T(8,128)(2,1)S(1)}, u32[]{:S(2)}, u32[]{:S(2)}) async-start(bf16[8,80,128]{2,1,0:T(8,128)(2,1)} %shard_map.67), calls=%async_computation.2 | async-start | bytes 327680 | tf_op jit(solution)/shard_map/all_to_all | solution.py:220
  64.3 0.1 pad_add_fusion.pos_ref
  64.4 5.3 %shard_map.64 = (bf16[2048,80]{1,0:T(8,128)(2,1)S(1)}, bf16[2048,80]{1,0:T(8,128)(2,1)S(1)}, bf16[80,2048]{1,0:T(8,128)(2,1)S(1)}, bf16[8,80,128]{2,1,0:T(8,128)(2,1)S(1)}, f32[8,1,128]{2,1,0:T(1,128)S(1)}) custom-call(bf16[8,240,128]{2,1,0:T(8,128)(2,1)S(1)} %pad_maximum_fusion.own_ref, bf16[8,240,128]{2,1,0:T(8,128)(2,1)S(1)} %collective-permute-done.3.oth_ref), custom_call_target="tpu_custom_call" | custom-call | flops 1342177280 | bytes 4000000 | tf_op jit(solution)/shard_map/pallas_call | solution.py:224
  69.7 5.7 %all-to-all-done.2.g_ref = bf16[8,80,128]{2,1,0:T(8,128)(2,1)S(1)} async-done(((bf16[8,80,128]{2,1,0:T(8,128)(2,1)}), bf16[8,80,128]{2,1,0:T(8,128)(2,1)S(1)}, u32[]{:S(2)}, u32[]{:S(2)}) %all-to-all-start.2) | async-done | bytes 163872 | tf_op jit(solution)/shard_map/all_to_all | solution.py:220
  75.4 3.6 %shard_map.68 = bf16[4,240,128]{2,1,0:T(8,128)(2,1)S(1)} custom-call(s32[3]{0:T(128)S(1)} %pad_add_fusion.pos_ref, bf16[8,240,128]{2,1,0:T(8,128)(2,1)S(1)} %pad_maximum_fusion.own_ref, bf16[2048,80]{1,0:T(8,128)(2,1)S(1)} %get-tuple-element.10.kr_ref, bf16[2048,80]{1,0:T(8,128)(2,1)S(1)} %get-tuple-element.11.vr_ref, ...), custom_call_target="tpu_custom_call" | custom-call | flops 1677721600 | bytes 4000000 | tf_op jit(solution)/shard_map/pallas_call | solution.py:239
  79.0 10.1 %all_to_all.20.in_ref = bf16[4,240,128]{2,1,0:T(8,128)(2,1)S(1)} all-to-all(bf16[4,240,128]{2,1,0:T(8,128)(2,1)S(1)} %shard_map.68), channel_id=1, replica_groups={{0,8,16,24},{32,40,48,56},{64,72,80,88},{96,104,112,120},{1,9,17,25},{3..., dimensions={0} | all-to-all | bytes 491520 | tf_op jit(solution)/shard_map/all_to_all | solution.py:242
  89.1 1.2 %shard_map.69 = bf16[3,160,128]{2,1,0:T(8,128)(2,1)} custom-call(s32[3]{0:T(128)S(1)} %pad_add_fusion.pos_ref, bf16[4,240,128]{2,1,0:T(8,128)(2,1)S(1)} %all_to_all.20.in_ref), custom_call_target="tpu_custom_call" | custom-call | flops 100000 | bytes 1000000 | tf_op jit(solution)/shard_map/pallas_call | solution.py:244
  (6 shorter events, 0.1 us)
Async XLA Ops:
  2.0 7.8 %copy-start.1 = (bf16[1,128,3,160]{1,3,2,0:T(8,128)(2,1)S(1)}, bf16[1,128,3,160]{1,3,2,0:T(8,128)(2,1)}, u32[]{:S(2)}) copy-start(bf16[1,128,3,160]{1,3,2,0:T(8,128)(2,1)} %param.6) | copy-start | bytes 368644
  2.0 24.4 %all-to-all-start = ((bf16[8,16,1280]{2,1,0:T(8,128)(2,1)}), bf16[8,16,1280]{2,1,0:T(8,128)(2,1)S(1)}, u32[]{:S(2)}, u32[]{:S(2)}) async-start(bf16[8,16,1280]{2,1,0:T(8,128)(2,1)} %shard_map.65), calls=%async_computation | async-start | bytes 655360 | tf_op jit(solution)/shard_map/all_to_all | solution.py:207
  9.8 5.6 %collective-permute-start = (bf16[240,128]{1,0:T(8,128)(2,1)S(1)}, bf16[240,128]{1,0:T(8,128)(2,1)S(1)}, u32[]{:S(2)}, u32[]{:S(2)}) collective-permute-start(bf16[240,128]{1,0:T(8,128)(2,1)S(1)} %bitcast.19), channel_id=1, source_target_pairs={{0,16},{8,24},{16,0},{24,8},{32,48},{40,56},{48,32},{56,40},{64,80... | collective-permute-start | bytes 184328 | tf_op jit(solution)/shard_map/ppermute | solution.py:195
  15.5 18.4 %collective-permute-start.1 = (bf16[2,240,128]{2,1,0:T(8,128)(2,1)S(1)}, bf16[2,240,128]{2,1,0:T(8,128)(2,1)S(1)}, u32[]{:S(2)}, u32[]{:S(2)}) collective-permute-start(bf16[2,240,128]{2,1,0:T(8,128)(2,1)S(1)} %pad_maximum_fusion.2), channel_id=1, source_target_pairs={{0,64},{8,72},{16,80},{24,88},{32,96},{40,104},{48,112},{56,120},{... | collective-permute-start | bytes 368648 | tf_op jit(solution)/shard_map/ppermute | solution.py:195
  27.2 26.8 %all-to-all-start.1 = ((bf16[8,16,1280]{2,1,0:T(8,128)(2,1)}), bf16[8,16,1280]{2,1,0:T(8,128)(2,1)S(1)}, u32[]{:S(2)}, u32[]{:S(2)}) async-start(bf16[8,16,1280]{2,1,0:T(8,128)(2,1)} %shard_map.66), calls=%async_computation.1 | async-start | bytes 655360 | tf_op jit(solution)/shard_map/all_to_all | solution.py:218
  33.8 20.1 %copy-start = (bf16[160,1280]{1,0:T(8,128)(2,1)S(1)}, bf16[160,1280]{1,0:T(8,128)(2,1)}, u32[]{:S(2)}) copy-start(bf16[160,1280]{1,0:T(8,128)(2,1)} %w_ref.1) | copy-start | bytes 1228804
  33.9 9.8 %collective-permute-start.2 = (bf16[4,240,128]{2,1,0:T(8,128)(2,1)S(1)}, bf16[4,240,128]{2,1,0:T(8,128)(2,1)S(1)}, u32[]{:S(2)}, u32[]{:S(2)}) collective-permute-start(bf16[4,240,128]{2,1,0:T(8,128)(2,1)S(1)} %pad_maximum_fusion.1), channel_id=1, source_target_pairs={{0,32},{8,40},{16,48},{24,56},{32,0},{40,8},{48,16},{56,24},{64,96... | collective-permute-start | bytes 737288 | tf_op jit(solution)/shard_map/ppermute | solution.py:195
  43.7 20.7 %collective-permute-start.3 = (bf16[8,240,128]{2,1,0:T(8,128)(2,1)S(1)}, bf16[8,240,128]{2,1,0:T(8,128)(2,1)S(1)}, u32[]{:S(2)}, u32[]{:S(2)}) collective-permute-start(bf16[8,240,128]{2,1,0:T(8,128)(2,1)S(1)} %pad_maximum_fusion.own_ref), channel_id=1, source_target_pairs={{0,8},{8,0},{16,24},{24,16},{32,40},{40,32},{48,56},{56,48},{64,72... | collective-permute-start | bytes 1474568 | tf_op jit(solution)/shard_map/ppermute | solution.py:195
  54.9 20.5 %all-to-all-start.2 = ((bf16[8,80,128]{2,1,0:T(8,128)(2,1)}), bf16[8,80,128]{2,1,0:T(8,128)(2,1)S(1)}, u32[]{:S(2)}, u32[]{:S(2)}) async-start(bf16[8,80,128]{2,1,0:T(8,128)(2,1)} %shard_map.67), calls=%async_computation.2 | async-start | bytes 327680 | tf_op jit(solution)/shard_map/all_to_all | solution.py:220
